TPU v7x, 256 devices: a whole 4x4x8 slice. The times are simulated.
256 devices in a mesh: sa: 4 (over y), row: 4 (over x), col: 16 (over z, core).
Axes of the slice: x: 4, y: 4, z: 8, core: 2. Of those that a mesh axis runs over, the one named last changes fastest.
Arguments:
- states: float32 [2560, 1024], P(None, 'sa')
- pool: float32 [32768, 1024], P(('row', 'col'), 'sa')
- pick: int32 [16384], P(('row', 'col')), may hold values from 0 to 32767, as said below
- tile_table: int32 [8256, 2], P(('row', 'col')), may hold values from 0 to 127, as said below
Outputs:
- normal_tiles: float32 [8256, 128, 128], P(('row', 'col'), 'sa')
Inputs may be any that keep to these rules, and one draw needn't show every extreme that they name: pick[m] lies in pool rows 2 * 256 * (m // 256) to 2 * 256 * (m // 256 + 1) - 1, and the picks of one such group of 256 centres are distinct. `tile_table`: each row (i, j) has i <= j; every such pair of blocks appears in exactly one row; a row stored on the device at index r of row and c of col names one block whose centres lie on a device at row index r and another whose centres lie on a device at col index c.
All inputs are finite; a program needn't handle non-finite values.
Results may differ from a plain program's by a relative error of at most 0.00033.
Values may be sent and summed in bfloat16 or wider, within the bound.
A program may use at most 128 MiB of HBM per device.

v0:
```python
import math
import jax
import jax.numpy as jnp
from jax import lax
from jax.sharding import PartitionSpec as P

F = 1024
M = 16384
MB = 128


def squared_gap(sample_part, centre_part):
    inner_part = jnp.dot(
        sample_part,
        centre_part.T,
        precision=lax.Precision.HIGHEST,
        preferred_element_type=jnp.float32,
    )
    sample_norms = jnp.sum(sample_part * sample_part, axis=1)[:, None]
    centre_norms = jnp.sum(centre_part * centre_part, axis=1)[None, :]
    return sample_norms + centre_norms - 2.0 * inner_part


def shards(states, pool, pick, tile_table):
    sample_count = states.shape[0]
    owner_index = lax.axis_index(("row", "col"))
    centres = jnp.take(pool, pick - owner_index * pool.shape[0], axis=0)
    wide_samples = lax.all_to_all(states, "sa", split_axis=0, concat_axis=1, tiled=True)
    wide_centres = lax.all_gather(centres, "sa", axis=1, tiled=True)
    distance = squared_gap(wide_samples, wide_centres)
    kernel = jnp.exp((2.0 * F - distance) / (4.0 * math.sqrt(F))).astype(jnp.bfloat16)
    kernel_panel = lax.all_gather(kernel, ("row", "col"), axis=1, tiled=True)
    panel_blocks = kernel_panel.reshape(kernel_panel.shape[0], M // MB, MB)
    tile_count = tile_table.shape[0]
    tile_groups = tile_table.reshape(3, tile_count // 3, 2)

    def products(tile_pairs):
        left_blocks = jnp.take(panel_blocks, tile_pairs[:, 0], axis=1)
        right_blocks = jnp.take(panel_blocks, tile_pairs[:, 1], axis=1)
        summed = jnp.einsum(
            "sga,sgb->gab", left_blocks, right_blocks, preferred_element_type=jnp.float32
        )
        return summed / sample_count

    partial_tiles = lax.map(products, tile_groups).reshape(tile_count, MB, MB)
    return lax.psum_scatter(partial_tiles, "sa", scatter_dimension=1, tiled=True)


def solution(mesh):
    placed = (P(None, "sa"), P(("row", "col"), "sa"), P(("row", "col")), P(("row", "col"), None))
    return jax.shard_map(
        shards, mesh=mesh, in_specs=placed, out_specs=P(("row", "col"), "sa", None), check_vma=False
    )
```

profile of v0, /device:TPU:1, one launch (start us, length us, event | category | flops | bytes accessed | tf_op | source)
XLA Modules:
  0.0 391.3 jit_solution(11058333592931336079)
XLA Ops:
  6.5 0.0 copy-start
  6.5 5.1 %all-to-all-start = ((f32[4,640,256]{2,1,0:T(8,128)}), f32[4,640,256]{2,1,0:T(8,128)S(1)}, u32[]{:S(2)}, u32[]{:S(2)}) async-start(f32[4,640,256]{2,1,0:T(8,128)} %bitcast.55), calls=%async_computation | async-start | bytes 5242880 | tf_op jit(solution)/shard_map/all_to_all | solution.py:28
  11.7 0.0 all-gather.3.cloned.1.call-start
  11.7 0.7 compare_and_fusion.2
  12.4 0.0 copy-done
  12.4 1.0 gather_fusion.2
  13.4 0.0 copy-start.2
  13.4 0.8 broadcast_select_fusion
  14.2 0.0 all-gather.3.cloned.1.call-update
  14.2 0.0 all-gather.5.cloned.1.call-start
  14.3 36.9 %all-gather.3.cloned.1.call-done = f32[256,1024]{1,0:T(8,128)} async-done(((f32[256,256]{1,0:T(8,128)}), f32[256,1024]{1,0:T(8,128)}) %all-gather.3.cloned.1.call-update) | async-done | bytes 1048592 | tf_op jit(solution)/shard_map/all_gather | solution.py:29
  51.2 1.4 multiply_reduce_fusion.1
  52.5 0.0 all-to-all-done
  52.5 2.1 copy.12
  54.7 0.2 multiply_reduce_fusion
  54.9 5.6 %fusion.18 = bf16[640,256]{0,1:T(8,128)(2,1)} fusion(f32[256,1024]{1,0:T(8,128)} %all-gather.3.cloned.1.call-done, f32[640,1024]{0,1:T(8,128)} %bitcast.53, f32[256]{0:T(256)S(1)} %multiply_reduce_fusion.1, f32[640]{0:T(1024)S(1)} %multiply_reduce_fusion), kind=kOutput, calls=%fused_computation.27 | convolution fusion | flops 2014248960 | bytes 4001280 | tf_op jit(solution)/shard_map/dot_general | solution.py:13
  60.6 0.0 all-gather.5.cloned.1.call-update
  60.6 0.0 reduce-scatter.2.cloned.1.call-start
  60.6 0.0 copy-done.2
  60.6 0.1 reshape.24
  60.7 112.9 %all-gather.5.cloned.1.call-done = bf16[640,16384]{0,1:T(8,128)(2,1)} async-done(((bf16[640,256]{0,1:T(8,128)(2,1)}), bf16[640,16384]{0,1:T(8,128)(2,1)}) %all-gather.5.cloned.1.call-update) | async-done | bytes 20971536 | tf_op jit(solution)/shard_map/all_gather | solution.py:32
  173.6 28.2 %copy.14 = bf16[640,128,128]{2,0,1:T(8,128)(2,1)} copy(bf16[640,128,128]{0,2,1:T(8,128)(2,1)} %bitcast.52) | data formatting | bytes 41943040 | tf_op jit(solution)/shard_map/while | solution.py:45
  201.8 102.5 %while.10 = (s32[]{:T(128)}, f32[3,43,128,128]{3,2,1,0:T(8,128)}, s32[3,43,2]{1,0,2:T(4,128)S(1)}, bf16[640,128,128]{2,0,1:T(8,128)(2,1)}, s32[]{:T(128)}) while((s32[]{:T(128)}, f32[3,43,128,128]{3,2,1,0:T(8,128)}, s32[3,43,2]{1,0,2:T(4,128)S(1)}, bf16[640,128,128]{2,0,1:T(8,128)(2,1)}, s32[]{:T(128)}) %tuple.32), condition=%wide.region_3.5_spmd, body=%wide.region_2.4_spmd.sunk | while | flops 909527552 | bytes 45099772 | solution.py:45
  201.8 12.5 %gather_fusion = bf16[43,640,128]{2,1,0:T(8,128)(2,1)} fusion(bf16[640,128,128]{2,0,1:T(8,128)(2,1)} %get-tuple-element.109, s32[1024]{0:T(1024)S(1)} %get-tuple-element.92), kind=kCustom, calls=%fused_computation.1.clone.clone.1 | custom fusion | bytes 14090412 | tf_op jit(solution)/shard_map/while/body/eval_jaxpr/jit(_take)/gather | solution.py:39
  214.3 12.4 %gather_fusion.1 = bf16[43,640,128]{2,1,0:T(8,128)(2,1)} fusion(bf16[640,128,128]{2,0,1:T(8,128)(2,1)} %get-tuple-element.109, s32[1024]{0:T(1024)S(1)} %get-tuple-element.94), kind=kCustom, calls=%fused_computation.clone.clone.1 | custom fusion | bytes 14090412 | tf_op jit(solution)/shard_map/while/body/eval_jaxpr/jit(_take)/gather | solution.py:38
  226.7 9.3 %bitcast_dynamic-update-slice_fusion.2 = f32[3,43,128,128]{3,2,1,0:T(8,128)} fusion(f32[3,43,128,128]{3,2,1,0:T(8,128)} %get-tuple-element.102, s32[]{:T(128)} %get-tuple-element.101, bf16[43,640,128]{2,1,0:T(8,128)(2,1)} %gather_fusion, pred[43]{0:T(512)(128)(4,1)S(1)} %get-tuple-element.93, bf16[43,640,128]{2,1,0:T(8,128)(2,1)} %gather_fusion.1, ...), kind=kOutput, calls=%fused_computation.11.clone.1 | convolution fusion | flops 909524992 | bytes 16908886 | tf_op jit(solution)/shard_map/while/body/eval_jaxpr/sga,sgb->gab/dot_general | solution.py:40
  236.0 12.4 %gather_fusion = bf16[43,640,128]{2,1,0:T(8,128)(2,1)} fusion(bf16[640,128,128]{2,0,1:T(8,128)(2,1)} %get-tuple-element.109, s32[1024]{0:T(1024)S(1)} %get-tuple-element.92), kind=kCustom, calls=%fused_computation.1.clone.clone.1 | custom fusion | bytes 14090412 | tf_op jit(solution)/shard_map/while/body/eval_jaxpr/jit(_take)/gather | solution.py:39
  248.4 12.4 %gather_fusion.1 = bf16[43,640,128]{2,1,0:T(8,128)(2,1)} fusion(bf16[640,128,128]{2,0,1:T(8,128)(2,1)} %get-tuple-element.109, s32[1024]{0:T(1024)S(1)} %get-tuple-element.94), kind=kCustom, calls=%fused_computation.clone.clone.1 | custom fusion | bytes 14090412 | tf_op jit(solution)/shard_map/while/body/eval_jaxpr/jit(_take)/gather | solution.py:38
  260.8 9.4 %bitcast_dynamic-update-slice_fusion.2 = f32[3,43,128,128]{3,2,1,0:T(8,128)} fusion(f32[3,43,128,128]{3,2,1,0:T(8,128)} %get-tuple-element.102, s32[]{:T(128)} %get-tuple-element.101, bf16[43,640,128]{2,1,0:T(8,128)(2,1)} %gather_fusion, pred[43]{0:T(512)(128)(4,1)S(1)} %get-tuple-element.93, bf16[43,640,128]{2,1,0:T(8,128)(2,1)} %gather_fusion.1, ...), kind=kOutput, calls=%fused_computation.11.clone.1 | convolution fusion | flops 909524992 | bytes 16908886 | tf_op jit(solution)/shard_map/while/body/eval_jaxpr/sga,sgb->gab/dot_general | solution.py:40
  270.3 12.5 %gather_fusion = bf16[43,640,128]{2,1,0:T(8,128)(2,1)} fusion(bf16[640,128,128]{2,0,1:T(8,128)(2,1)} %get-tuple-element.109, s32[1024]{0:T(1024)S(1)} %get-tuple-element.92), kind=kCustom, calls=%fused_computation.1.clone.clone.1 | custom fusion | bytes 14090412 | tf_op jit(solution)/shard_map/while/body/eval_jaxpr/jit(_take)/gather | solution.py:39
  282.7 12.4 %gather_fusion.1 = bf16[43,640,128]{2,1,0:T(8,128)(2,1)} fusion(bf16[640,128,128]{2,0,1:T(8,128)(2,1)} %get-tuple-element.109, s32[1024]{0:T(1024)S(1)} %get-tuple-element.94), kind=kCustom, calls=%fused_computation.clone.clone.1 | custom fusion | bytes 14090412 | tf_op jit(solution)/shard_map/while/body/eval_jaxpr/jit(_take)/gather | solution.py:38
  295.1 9.3 %bitcast_dynamic-update-slice_fusion.2 = f32[3,43,128,128]{3,2,1,0:T(8,128)} fusion(f32[3,43,128,128]{3,2,1,0:T(8,128)} %get-tuple-element.102, s32[]{:T(128)} %get-tuple-element.101, bf16[43,640,128]{2,1,0:T(8,128)(2,1)} %gather_fusion, pred[43]{0:T(512)(128)(4,1)S(1)} %get-tuple-element.93, bf16[43,640,128]{2,1,0:T(8,128)(2,1)} %gather_fusion.1, ...), kind=kOutput, calls=%fused_computation.11.clone.1 | convolution fusion | flops 909524992 | bytes 16908886 | tf_op jit(solution)/shard_map/while/body/eval_jaxpr/sga,sgb->gab/dot_general | solution.py:40
  304.3 0.0 copy-start.1
  304.3 0.0 reduce-scatter.2.cloned.1.call-update
  304.4 80.4 %reduce-scatter.2.cloned.1.call-done = f32[129,32,128]{2,1,0:T(8,128)} async-done(((f32[129,128,128]{2,1,0:T(8,128)}), f32[129,32,128]{2,1,0:T(8,128)}) %reduce-scatter.2.cloned.1.call-update) | async-done | bytes 2113552 | tf_op jit(solution)/shard_map/reduce_scatter | solution.py:46
  384.8 0.0 copy-done.1
  (11 shorter events, 0.1 us)
Async XLA Ops:
  6.5 5.8 %copy-start = (f32[512,256]{1,0:T(8,128)S(1)}, f32[512,256]{1,0:T(8,128)}, u32[]{:S(2)}) copy-start(f32[512,256]{1,0:T(8,128)} %param.9) | copy-start | bytes 1572868
  6.5 46.0 %all-to-all-start = ((f32[4,640,256]{2,1,0:T(8,128)}), f32[4,640,256]{2,1,0:T(8,128)S(1)}, u32[]{:S(2)}, u32[]{:S(2)}) async-start(f32[4,640,256]{2,1,0:T(8,128)} %bitcast.55), calls=%async_computation | async-start | bytes 5242880 | tf_op jit(solution)/shard_map/all_to_all | solution.py:28
  11.7 39.5 %all-gather.3.cloned.1.call-start = ((), (), s32[]{:S(2)}) async-start(), calls=%async_computation.2 | async-start | bytes 1310720 | tf_op jit(solution)/shard_map/all_gather | solution.py:29
  13.4 47.3 %copy-start.2 = (s32[129,2]{0,1:T(2,128)S(1)}, s32[129,2]{0,1:T(2,128)}, u32[]{:S(2)}) copy-start(s32[129,2]{0,1:T(2,128)} %param.11) | copy-start | bytes 3100
  14.2 159.4 %all-gather.5.cloned.1.call-start = ((), (), s32[]{:S(2)}) async-start(), calls=%async_computation.3 | async-start | bytes 21299200 | tf_op jit(solution)/shard_map/all_gather | solution.py:32
  60.6 324.2 %reduce-scatter.2.cloned.1.call-start = ((), (), s32[]{:S(2)}) async-start(), calls=%async_computation.4 | async-start | bytes 10567680 | tf_op jit(solution)/shard_map/reduce_scatter | solution.py:46
  304.3 80.4 %copy-start.1 = (f32[512,256]{1,0:T(8,128)S(1)}, f32[512,256]{1,0:T(8,128)}, u32[]{:S(2)}) copy-start(f32[512,256]{1,0:T(8,128)} %param.9) | copy-start | bytes 1572868
Sparse Core Ops, SparseCore 0:
  14.3 36.7 all-gather.2
  60.7 112.8 all-gather.4
  304.5 80.2 reduce-scatter.1
where the time goes:
time: 392 us; the launch traced here: 391 us
  waiting for transfers between devices  230 us (59%)
  local copies, waits for them, and re-layouts  106 us (27%)
  matrix products  33.6 us (9%)
  between operations  13.2 us (3%)
  starting transfers between devices  5.23 us (1%)
    all_gather x1, waiting for transfers between devices, shards(): kernel_panel = lax.all_gather(kernel, ('row', 'col'), axis=1, tiled=True)  113 us
    reduce_scatter x1, waiting for transfers between devices, shards(): lax.psum_scatter(partial_tiles, 'sa', scatter_dimension=1, tiled=True)  80.4 us
    gather x3, local copies, waits for them, and re-layouts, products(): right_blocks = jnp.take(panel_blocks, tile_pairs[:, 1], axis=1)  37.3 us
    gather x3, local copies, waits for them, and re-layouts, products(): left_blocks = jnp.take(panel_blocks, tile_pairs[:, 0], axis=1)  37.1 us
    all_gather x1, waiting for transfers between devices, shards(): wide_centres = lax.all_gather(centres, 'sa', axis=1, tiled=True)  36.9 us
    while x1, local copies, waits for them, and re-layouts, shards(): partial_tiles = lax.map(products, tile_groups).reshape(tile_count, MB, MB)  28.2 us
    dot_general x3, matrix products, products(): jnp.einsum('sga,sgb->gab', left_blocks, right_blocks, preferred_element_t...  28 us
  transfers between devices with their start and end apart: 4, of which 3 were waited for; matrix products, arithmetic and copies ran while one was open for 1% of the time, Pallas kernels for 0%

commit v1 on v0

--- a/solution.py
+++ b/solution.py
@@ -29,7 +29,10 @@
     wide_centres = lax.all_gather(centres, "sa", axis=1, tiled=True)
     distance = squared_gap(wide_samples, wide_centres)
     kernel = jnp.exp((2.0 * F - distance) / (4.0 * math.sqrt(F))).astype(jnp.bfloat16)
-    kernel_panel = lax.all_gather(kernel, ("row", "col"), axis=1, tiled=True)
+    kernel_panel = jnp.concatenate(
+        lax.all_to_all(jnp.stack(lax.axis_size(("row", "col")) * [kernel]), ("row", "col"), 0, 0),
+        axis=1,
+    )
     panel_blocks = kernel_panel.reshape(kernel_panel.shape[0], M // MB, MB)
     tile_count = tile_table.shape[0]
     tile_groups = tile_table.reshape(3, tile_count // 3, 2)

time: 392 us -> 754 us (1.92)
  waiting for transfers between devices: 230 us -> 573 us
  starting transfers between devices: 5.23 us -> 17.4 us
    all_to_all x0 -> x1, waiting for transfers between devices: none -> 456 us  [shards(): lax.all_to_all(jnp.stack(lax.axis_size(('row', 'col')) * [kernel]), ('row...]
    all_gather x1 -> x0, waiting for transfers between devices: 113 us -> none  [shards(): kernel_panel = lax.all_gather(kernel, ('row', 'col'), axis=1, tiled=True)]
    all_to_all x0 -> x1, starting transfers between devices: none -> 12.2 us  [shards(): lax.all_to_all(jnp.stack(lax.axis_size(('row', 'col')) * [kernel]), ('row...]
    another operation x0 -> x1, local copies, waits for them, and re-layouts: none -> 7.94 us  [shards(): jnp.stack(lax.axis_size(('row', 'col')) * [kernel])]
where the time goes in v1:
time: 754 us; the launch traced here: 753 us
  waiting for transfers between devices  573 us (76%)
  local copies, waits for them, and re-layouts  113 us (15%)
  matrix products  32.9 us (4%)
  starting transfers between devices  17.4 us (2%)
  between operations  13.5 us (2%)
    all_to_all x1, waiting for transfers between devices, shards(): lax.all_to_all(jnp.stack(lax.axis_size(('row', 'col')) * [kernel]), ('row...  456 us
    reduce_scatter x1, waiting for transfers between devices, shards(): lax.psum_scatter(partial_tiles, 'sa', scatter_dimension=1, tiled=True)  80.5 us
    gather x3, local copies, waits for them, and re-layouts, products(): right_blocks = jnp.take(panel_blocks, tile_pairs[:, 1], axis=1)  37.4 us
    gather x3, local copies, waits for them, and re-layouts, products(): left_blocks = jnp.take(panel_blocks, tile_pairs[:, 0], axis=1)  37.1 us
    all_gather x1, waiting for transfers between devices, shards(): wide_centres = lax.all_gather(centres, 'sa', axis=1, tiled=True)  37 us
    dot_general x3, matrix products, products(): jnp.einsum('sga,sgb->gab', left_blocks, right_blocks, preferred_element_t...  28 us
    while x1, local copies, waits for them, and re-layouts, shards(): partial_tiles = lax.map(products, tile_groups).reshape(tile_count, MB, MB)  27 us
  transfers between devices with their start and end apart: 4, of which 3 were waited for; matrix products, arithmetic and copies ran while one was open for 1% of the time, Pallas kernels for 0%

profile of v1, /device:TPU:1, one launch (start us, length us, event | category | flops | bytes accessed | tf_op | source)
XLA Modules:
  0.0 752.7 jit_solution(17656121695447394426)
XLA Ops:
  6.5 0.0 copy-start
  6.5 5.1 all-to-all-start
  11.7 0.0 all-gather.2.cloned.1.call-start
  11.7 0.7 compare_and_fusion.2
  12.4 0.0 copy-done
  12.4 1.0 gather_fusion.2
  13.4 0.8 broadcast_select_fusion
  14.2 0.0 all-gather.2.cloned.1.call-update
  14.2 37.0 %all-gather.2.cloned.1.call-done = f32[256,1024]{1,0:T(8,128)} async-done(((f32[256,256]{1,0:T(8,128)}), f32[256,1024]{1,0:T(8,128)}) %all-gather.2.cloned.1.call-update) | async-done | bytes 1048592 | tf_op jit(solution)/shard_map/all_gather | solution.py:29
  51.2 1.4 multiply_reduce_fusion.1
  52.5 0.0 all-to-all-done
  52.5 2.1 copy.12
  54.7 0.2 multiply_reduce_fusion
  54.9 4.9 fusion.18
  59.8 7.9 %stack.2 = bf16[64,640,256]{1,2,0:T(8,128)(2,1)} broadcast(bf16[640,256]{0,1:T(8,128)(2,1)S(1)} %fusion.18), dimensions={1,2} | broadcast | bytes 21299200 | tf_op jit(solution)/shard_map/stack | solution.py:33
  67.8 0.0 copy-start.2
  67.8 12.2 %all-to-all-start.1 = ((bf16[64,640,256]{1,2,0:T(8,128)(2,1)}), bf16[64,640,256]{1,2,0:T(8,128)(2,1)}, u32[]{:S(2)}, u32[]{:S(2)}) async-start(bf16[64,640,256]{1,2,0:T(8,128)(2,1)} %stack.2), calls=%async_computation.1 | async-start | bytes 41943040 | tf_op jit(solution)/shard_map/all_to_all | solution.py:33
  80.0 0.0 reduce-scatter.2.cloned.1.call-start
  80.1 0.0 copy-done.2
  80.1 0.1 reshape.26
  80.2 455.6 %all-to-all-done.1 = bf16[64,640,256]{1,2,0:T(8,128)(2,1)} async-done(((bf16[64,640,256]{1,2,0:T(8,128)(2,1)}), bf16[64,640,256]{1,2,0:T(8,128)(2,1)}, u32[]{:S(2)}, u32[]{:S(2)}) %all-to-all-start.1) | async-done | bytes 20971552 | tf_op jit(solution)/shard_map/all_to_all | solution.py:33
  535.8 27.0 %copy.14 = bf16[640,128,128]{2,0,1:T(8,128)(2,1)} copy(bf16[640,128,128]{0,2,1:T(8,128)(2,1)} %bitcast.11) | data formatting | bytes 41943040 | tf_op jit(solution)/shard_map/while | solution.py:48
  562.8 102.5 %while.10 = (s32[]{:T(128)}, f32[3,43,128,128]{3,2,1,0:T(8,128)}, s32[3,43,2]{1,0,2:T(4,128)S(1)}, bf16[640,128,128]{2,0,1:T(8,128)(2,1)}, s32[]{:T(128)}) while((s32[]{:T(128)}, f32[3,43,128,128]{3,2,1,0:T(8,128)}, s32[3,43,2]{1,0,2:T(4,128)S(1)}, bf16[640,128,128]{2,0,1:T(8,128)(2,1)}, s32[]{:T(128)}) %tuple.31), condition=%wide.region_3.5_spmd, body=%wide.region_2.4_spmd.sunk | while | flops 909527552 | bytes 45099772 | solution.py:48
  562.8 12.5 %gather_fusion = bf16[43,640,128]{2,1,0:T(8,128)(2,1)} fusion(bf16[640,128,128]{2,0,1:T(8,128)(2,1)} %get-tuple-element.105, s32[1024]{0:T(1024)S(1)} %get-tuple-element.88), kind=kCustom, calls=%fused_computation.1.clone.clone.1 | custom fusion | bytes 14090412 | tf_op jit(solution)/shard_map/while/body/eval_jaxpr/jit(_take)/gather | solution.py:42
  575.3 12.4 %gather_fusion.1 = bf16[43,640,128]{2,1,0:T(8,128)(2,1)} fusion(bf16[640,128,128]{2,0,1:T(8,128)(2,1)} %get-tuple-element.105, s32[1024]{0:T(1024)S(1)} %get-tuple-element.90), kind=kCustom, calls=%fused_computation.clone.clone.1 | custom fusion | bytes 14090412 | tf_op jit(solution)/shard_map/while/body/eval_jaxpr/jit(_take)/gather | solution.py:41
  587.7 9.3 %bitcast_dynamic-update-slice_fusion.2 = f32[3,43,128,128]{3,2,1,0:T(8,128)} fusion(f32[3,43,128,128]{3,2,1,0:T(8,128)} %get-tuple-element.98, s32[]{:T(128)} %get-tuple-element.97, bf16[43,640,128]{2,1,0:T(8,128)(2,1)} %gather_fusion, pred[43]{0:T(512)(128)(4,1)S(1)} %get-tuple-element.89, bf16[43,640,128]{2,1,0:T(8,128)(2,1)} %gather_fusion.1, ...), kind=kOutput, calls=%fused_computation.11.clone.1 | convolution fusion | flops 909524992 | bytes 16908886 | tf_op jit(solution)/shard_map/while/body/eval_jaxpr/sga,sgb->gab/dot_general | solution.py:43
  597.0 12.4 %gather_fusion = bf16[43,640,128]{2,1,0:T(8,128)(2,1)} fusion(bf16[640,128,128]{2,0,1:T(8,128)(2,1)} %get-tuple-element.105, s32[1024]{0:T(1024)S(1)} %get-tuple-element.88), kind=kCustom, calls=%fused_computation.1.clone.clone.1 | custom fusion | bytes 14090412 | tf_op jit(solution)/shard_map/while/body/eval_jaxpr/jit(_take)/gather | solution.py:42
  609.4 12.4 %gather_fusion.1 = bf16[43,640,128]{2,1,0:T(8,128)(2,1)} fusion(bf16[640,128,128]{2,0,1:T(8,128)(2,1)} %get-tuple-element.105, s32[1024]{0:T(1024)S(1)} %get-tuple-element.90), kind=kCustom, calls=%fused_computation.clone.clone.1 | custom fusion | bytes 14090412 | tf_op jit(solution)/shard_map/while/body/eval_jaxpr/jit(_take)/gather | solution.py:41
  621.8 9.4 %bitcast_dynamic-update-slice_fusion.2 = f32[3,43,128,128]{3,2,1,0:T(8,128)} fusion(f32[3,43,128,128]{3,2,1,0:T(8,128)} %get-tuple-element.98, s32[]{:T(128)} %get-tuple-element.97, bf16[43,640,128]{2,1,0:T(8,128)(2,1)} %gather_fusion, pred[43]{0:T(512)(128)(4,1)S(1)} %get-tuple-element.89, bf16[43,640,128]{2,1,0:T(8,128)(2,1)} %gather_fusion.1, ...), kind=kOutput, calls=%fused_computation.11.clone.1 | convolution fusion | flops 909524992 | bytes 16908886 | tf_op jit(solution)/shard_map/while/body/eval_jaxpr/sga,sgb->gab/dot_general | solution.py:43
  631.3 12.5 %gather_fusion = bf16[43,640,128]{2,1,0:T(8,128)(2,1)} fusion(bf16[640,128,128]{2,0,1:T(8,128)(2,1)} %get-tuple-element.105, s32[1024]{0:T(1024)S(1)} %get-tuple-element.88), kind=kCustom, calls=%fused_computation.1.clone.clone.1 | custom fusion | bytes 14090412 | tf_op jit(solution)/shard_map/while/body/eval_jaxpr/jit(_take)/gather | solution.py:42
  643.7 12.4 %gather_fusion.1 = bf16[43,640,128]{2,1,0:T(8,128)(2,1)} fusion(bf16[640,128,128]{2,0,1:T(8,128)(2,1)} %get-tuple-element.105, s32[1024]{0:T(1024)S(1)} %get-tuple-element.90), kind=kCustom, calls=%fused_computation.clone.clone.1 | custom fusion | bytes 14090412 | tf_op jit(solution)/shard_map/while/body/eval_jaxpr/jit(_take)/gather | solution.py:41
  656.1 9.3 %bitcast_dynamic-update-slice_fusion.2 = f32[3,43,128,128]{3,2,1,0:T(8,128)} fusion(f32[3,43,128,128]{3,2,1,0:T(8,128)} %get-tuple-element.98, s32[]{:T(128)} %get-tuple-element.97, bf16[43,640,128]{2,1,0:T(8,128)(2,1)} %gather_fusion, pred[43]{0:T(512)(128)(4,1)S(1)} %get-tuple-element.89, bf16[43,640,128]{2,1,0:T(8,128)(2,1)} %gather_fusion.1, ...), kind=kOutput, calls=%fused_computation.11.clone.1 | convolution fusion | flops 909524992 | bytes 16908886 | tf_op jit(solution)/shard_map/while/body/eval_jaxpr/sga,sgb->gab/dot_general | solution.py:43
  665.3 0.0 copy-start.1
  665.3 0.0 reduce-scatter.2.cloned.1.call-update
  665.4 80.5 %reduce-scatter.2.cloned.1.call-done = f32[129,32,128]{2,1,0:T(8,128)} async-done(((f32[129,128,128]{2,1,0:T(8,128)}), f32[129,32,128]{2,1,0:T(8,128)}) %reduce-scatter.2.cloned.1.call-update) | async-done | bytes 2113552 | tf_op jit(solution)/shard_map/reduce_scatter | solution.py:49
  745.9 0.0 copy-done.1
  (11 shorter events, 0.1 us)
Async XLA Ops:
  6.5 5.8 copy-start
  6.5 46.0 %all-to-all-start = ((f32[4,640,256]{2,1,0:T(8,128)}), f32[4,640,256]{2,1,0:T(8,128)S(1)}, u32[]{:S(2)}, u32[]{:S(2)}) async-start(f32[4,640,256]{2,1,0:T(8,128)} %bitcast.56), calls=%async_computation | async-start | bytes 5242880 | tf_op jit(solution)/shard_map/all_to_all | solution.py:28
  11.7 39.5 %all-gather.2.cloned.1.call-start = ((), (), s32[]{:S(2)}) async-start(), calls=%async_computation.3 | async-start | bytes 1310720 | tf_op jit(solution)/shard_map/all_gather | solution.py:29
  67.8 12.3 %copy-start.2 = (s32[129,2]{0,1:T(2,128)S(1)}, s32[129,2]{0,1:T(2,128)}, u32[]{:S(2)}) copy-start(s32[129,2]{0,1:T(2,128)} %param.11) | copy-start | bytes 3100
  67.8 468.0 %all-to-all-start.1 = ((bf16[64,640,256]{1,2,0:T(8,128)(2,1)}), bf16[64,640,256]{1,2,0:T(8,128)(2,1)}, u32[]{:S(2)}, u32[]{:S(2)}) async-start(bf16[64,640,256]{1,2,0:T(8,128)(2,1)} %stack.2), calls=%async_computation.1 | async-start | bytes 41943040 | tf_op jit(solution)/shard_map/all_to_all | solution.py:33
  80.0 665.8 %reduce-scatter.2.cloned.1.call-start = ((), (), s32[]{:S(2)}) async-start(), calls=%async_computation.4 | async-start | bytes 10567680 | tf_op jit(solution)/shard_map/reduce_scatter | solution.py:49
  665.3 80.5 %copy-start.1 = (f32[512,256]{1,0:T(8,128)S(1)}, f32[512,256]{1,0:T(8,128)}, u32[]{:S(2)}) copy-start(f32[512,256]{1,0:T(8,128)} %param.9) | copy-start | bytes 1572868
Sparse Core Ops, SparseCore 0:
  14.3 36.8 all-gather.1
  665.5 80.3 reduce-scatter.1
